TPU v7x, 32 devices: a whole 2x2x4 slice. The times are simulated.
32 devices in a mesh: probe: 16 (over z, y, core), strip: 2 (over x).
Axes of the slice: x: 2, y: 2, z: 4, core: 2. Of those that a mesh axis runs over, the one named last changes fastest.
Arguments:
- potential: float32 [2, 512, 2048], P(None, 'probe', 'strip'), may hold values from 0 to 2
- probe_wave: float32 [2, 256, 256], replicated, may hold values from -6 to 6
- offsets: int32 [2, 2, 96], P('strip'), may hold values from -128 to 896, as said below
- members: int32 [2, 16, 6], P('strip', 'probe'), may hold values from 0 to 95, as said below
- counts: int32 [2, 16], P('strip', 'probe'), may hold values from 1 to 6, as said below
- measured: float32 [2, 16, 6, 256, 256], P('strip', 'probe'), may hold values from 0 to 4
Outputs:
- potential_grad: float32 [2, 512, 2048], P(None, 'probe', 'strip')
Inputs may be any that keep to these rules, and one draw needn't show every extreme that they name: offsets[s, 0, p] is a window's first row, 0 to 256; offsets[s, 1, p] its first column counted from the strip's first column, -128 to 896; both ends of both ranges occur in every strip. `members`: every position of a strip is listed exactly once over that strip's groups; a group uses its first counts[s, g] entries. `counts`: in every strip some group uses all 6 slots and some group uses one.
All inputs are finite; a program needn't handle non-finite values.
Results may differ from a plain program's by a relative error of at most 0.00021.
Values sent between devices are 32-bit elements; how exact they have to be, the bound alone decides.
No kernel may reach another device: no remote copies, remote signals or barrier semaphores. Data moves between devices by JAX's collectives and lax.ppermute only.
A program may use at most 64 MiB of HBM per device.

v0:
```python
import math
import jax
import jax.numpy as jnp
from jax import lax
from jax.sharding import PartitionSpec as P

EDGE = 128
A_PROP = 0.1
LOSS_SCALE = 0.03125


def extended(value, sides, width):
    for axis, dim in sides:
        peers, length = (lax.axis_size(axis), value.shape[dim])
        up = [(i, (i + 1) % peers) for i in range(peers - 1)]
        down = [(j, i) for i, j in up]
        last = lax.slice_in_dim(value, length - width, length, axis=dim)
        initial = lax.slice_in_dim(value, 0, width, axis=dim)
        before = lax.ppermute(last, axis, up)
        after = lax.ppermute(initial, axis, down)
        value = jnp.concatenate([before, value, after], axis=dim)
    return value


def laplace(values):
    padded = jnp.pad(values, ((1, 1), (1, 1)))
    return (
        padded[2:, 1:-1] + padded[:-2, 1:-1] + padded[1:-1, 2:] + padded[1:-1, :-2] - 4.0 * values
    )


def propagate(real_part, imag_part):
    term_re, term_im = (real_part, imag_part)
    out_re, out_im = (real_part, imag_part)
    for degree in range(1, 5):
        lap_re = laplace(term_re)
        lap_im = laplace(term_im)
        term_re, term_im = (-A_PROP / degree * lap_im, A_PROP / degree * lap_re)
        out_re = out_re + term_re
        out_im = out_im + term_im
    return (out_re, out_im)


def exit_wave(window, probe_wave):
    real_part, imag_part = (probe_wave[0], probe_wave[1])
    for slice_index in range(window.shape[0]):
        phases = window[slice_index]
        cosine, sine_part = (jnp.cos(phases), jnp.sin(phases))
        real_part, imag_part = (
            real_part * cosine - imag_part * sine_part,
            real_part * sine_part + imag_part * cosine,
        )
        real_part, imag_part = propagate(real_part, imag_part)
    return (real_part, imag_part)


def dft_tables(window_size):
    indices = jnp.arange(window_size, dtype=jnp.int32)
    product = indices[:, None] * indices[None, :] % window_size
    angles = -2.0 * math.pi / window_size * product.astype(jnp.float32)
    normal_scale = 1.0 / math.sqrt(window_size)
    return (jnp.cos(angles) * normal_scale, jnp.sin(angles) * normal_scale)


def matmul(left_side, right_side):
    return jnp.dot(
        left_side, right_side, precision=lax.Precision.HIGHEST, preferred_element_type=jnp.float32
    )


def slot_loss(window, probe_wave, intensity_data, table_re, table_im):
    real_part, imag_part = exit_wave(window, probe_wave)
    inner_re = matmul(table_re, real_part) - matmul(table_im, imag_part)
    inner_im = matmul(table_re, imag_part) + matmul(table_im, real_part)
    far_re = matmul(inner_re, table_re) - matmul(inner_im, table_im)
    far_im = matmul(inner_re, table_im) + matmul(inner_im, table_re)
    intensity = far_re * far_re + far_im * far_im
    return LOSS_SCALE * jnp.sum((intensity - intensity_data) ** 2)


def split_edges(gradient, own_width):
    outgoing = jnp.concatenate([gradient[:, :, :EDGE], gradient[:, :, own_width + EDGE :]], axis=2)
    return (outgoing, gradient[:, :, EDGE : EDGE + own_width])


def add_edges(own_part, arrived, own_width):
    own_part = own_part.at[:, :, :EDGE].add(arrived[:, :, :EDGE])
    return own_part.at[:, :, own_width - EDGE :].add(arrived[:, :, 3 * EDGE :])


def shards(potential, probe_wave, offsets, members, counts, measured):
    own_width = potential.shape[2]
    widened = extended(potential, (("strip", 2),), EDGE)
    whole_object = lax.all_gather(widened, "probe", axis=1, tiled=True)
    window_size = probe_wave.shape[-1]
    table_re, table_im = dft_tables(window_size)
    anchor = jnp.zeros((), jnp.int32)
    loss_grad = jax.grad(slot_loss)

    def visit(slot_index, gradient):
        position = members[0, 0, slot_index]
        start_row = offsets[0, 0, position]
        start_column = offsets[0, 1, position] + EDGE
        window = lax.dynamic_slice(
            whole_object,
            (anchor, start_row, start_column),
            (whole_object.shape[0], window_size, window_size),
        )
        window_grad = loss_grad(window, probe_wave, measured[0, 0, slot_index], table_re, table_im)
        current = lax.dynamic_slice(gradient, (anchor, start_row, start_column), window.shape)
        return lax.dynamic_update_slice(
            gradient, current + window_grad, (anchor, start_row, start_column)
        )

    gradient = lax.fori_loop(0, counts[0, 0], visit, jnp.zeros(whole_object.shape, jnp.float32))
    outgoing, own_part = split_edges(gradient, own_width)
    arrived = extended(outgoing, (("strip", 2),), EDGE)
    folded = add_edges(own_part, arrived, own_width)
    return lax.psum_scatter(folded, "probe", scatter_dimension=1, tiled=True)


def solution(mesh):
    placed = (
        P(None, "probe", "strip"),
        P(),
        P("strip", None, None),
        P("strip", "probe", None),
        P("strip", "probe"),
        P("strip", "probe", None, None, None),
    )
    return jax.shard_map(
        shards, mesh=mesh, in_specs=placed, out_specs=P(None, "probe", "strip"), check_vma=False
    )
```

profile of v0, /device:TPU:0, one launch (start us, length us, event | category | flops | bytes accessed | tf_op | source)
XLA Modules:
  0.0 486.8 jit_solution(17927370276558367795)
XLA Ops:
  7.3 4.9 collective-permute-start
  13.8 4.2 collective-permute-done.1
  21.3 54.9 %all-gather.2.cloned.1.call-done = f32[2,512,1280]{2,0,1:T(2,128)} async-done(((f32[2,32,1280]{2,0,1:T(2,128)}), f32[2,512,1280]{2,0,1:T(2,128)}) %all-gather.2.cloned.1.call-update) | async-done | bytes 5242896 | tf_op jit(solution)/shard_map/all_gather | solution.py:94
  76.2 2.7 broadcast_in_dim.28.clone
  79.0 308.3 %while.17 = (s32[]{:T(128)}, f32[2,512,1280]{2,1,0:T(8,128)}, s32[]{:T(128)}, s32[1,1,6]{2,1,0:T(1,128)S(1)}, s32[1,2,96]{2,1,0:T(2,128)S(1)}, /*index=5*/f32[2,...) while((s32[]{:T(128)}, f32[2,512,1280]{2,1,0:T(8,128)}, ...), condition=%wide.region_1.2_spmd.clone.clone, body=%wide.region_0.1_spmd.clone.clone.sunk | while | flops 3259498496 | bytes 60293496 | solution.py:115
  85.9 2.6 fusion.321
  102.8 1.5 fusion.330
  104.3 1.5 convolution_add_fusion.11
  105.8 2.5 add_multiply_fusion.3
  113.7 1.5 fusion.336
  115.2 1.5 fusion.334
  116.7 1.5 broadcast_multiply_fusion.41
  118.2 1.5 fusion.337
  123.6 6.6 %dynamic_update_slice.10 = f32[2,512,1280]{2,1,0:T(8,128)} dynamic-update-slice(f32[2,512,1280]{2,1,0:T(8,128)} %get-tuple-element.599, f32[2,256,256]{2,1,0:T(8,128)S(1)} %copy.35, s32[]{:T(128)} %constant.243.clone.1..sunk, s32[]{:T(128)S(6)} %select_n.157, s32[]{:T(128)S(6)} %select_n.158) | dynamic-update-slice | bytes 1048580 | tf_op jit(solution)/shard_map/while/body/dynamic_update_slice | solution.py:111
  137.2 2.6 fusion.321
  152.6 1.5 fusion.332
  154.1 1.5 fusion.330
  155.6 1.5 convolution_add_fusion.11
  157.1 2.5 add_multiply_fusion.3
  165.0 1.5 fusion.336
  166.5 1.5 fusion.334
  168.0 1.5 broadcast_multiply_fusion.41
  169.5 1.5 fusion.337
  174.9 6.4 %dynamic_update_slice.10 = f32[2,512,1280]{2,1,0:T(8,128)} dynamic-update-slice(f32[2,512,1280]{2,1,0:T(8,128)} %get-tuple-element.599, f32[2,256,256]{2,1,0:T(8,128)S(1)} %copy.35, s32[]{:T(128)} %constant.243.clone.1..sunk, s32[]{:T(128)S(6)} %select_n.157, s32[]{:T(128)S(6)} %select_n.158) | dynamic-update-slice | bytes 1048580 | tf_op jit(solution)/shard_map/while/body/dynamic_update_slice | solution.py:111
  188.2 2.7 fusion.321
  205.3 1.5 fusion.330
  206.8 1.5 convolution_add_fusion.11
  208.3 2.5 add_multiply_fusion.3
  216.3 1.5 fusion.336
  217.8 1.5 fusion.334
  219.3 1.5 broadcast_multiply_fusion.41
  220.7 1.5 fusion.337
  226.2 6.1 %dynamic_update_slice.10 = f32[2,512,1280]{2,1,0:T(8,128)} dynamic-update-slice(f32[2,512,1280]{2,1,0:T(8,128)} %get-tuple-element.599, f32[2,256,256]{2,1,0:T(8,128)S(1)} %copy.35, s32[]{:T(128)} %constant.243.clone.1..sunk, s32[]{:T(128)S(6)} %select_n.157, s32[]{:T(128)S(6)} %select_n.158) | dynamic-update-slice | bytes 1048580 | tf_op jit(solution)/shard_map/while/body/dynamic_update_slice | solution.py:111
  239.2 2.7 fusion.321
  256.3 1.5 fusion.330
  257.7 1.5 convolution_add_fusion.11
  259.2 2.5 add_multiply_fusion.3
  267.2 1.5 fusion.336
  270.2 1.5 broadcast_multiply_fusion.41
  271.6 1.5 fusion.337
  277.1 6.6 %dynamic_update_slice.10 = f32[2,512,1280]{2,1,0:T(8,128)} dynamic-update-slice(f32[2,512,1280]{2,1,0:T(8,128)} %get-tuple-element.599, f32[2,256,256]{2,1,0:T(8,128)S(1)} %copy.35, s32[]{:T(128)} %constant.243.clone.1..sunk, s32[]{:T(128)S(6)} %select_n.157, s32[]{:T(128)S(6)} %select_n.158) | dynamic-update-slice | bytes 1048580 | tf_op jit(solution)/shard_map/while/body/dynamic_update_slice | solution.py:111
  290.7 2.7 fusion.321
  307.7 1.5 fusion.330
  309.2 1.5 convolution_add_fusion.11
  310.7 2.5 add_multiply_fusion.3
  318.7 1.5 fusion.336
  320.2 1.5 fusion.334
  321.6 1.5 broadcast_multiply_fusion.41
  323.1 1.5 fusion.337
  328.6 6.5 %dynamic_update_slice.10 = f32[2,512,1280]{2,1,0:T(8,128)} dynamic-update-slice(f32[2,512,1280]{2,1,0:T(8,128)} %get-tuple-element.599, f32[2,256,256]{2,1,0:T(8,128)S(1)} %copy.35, s32[]{:T(128)} %constant.243.clone.1..sunk, s32[]{:T(128)S(6)} %select_n.157, s32[]{:T(128)S(6)} %select_n.158) | dynamic-update-slice | bytes 1048580 | tf_op jit(solution)/shard_map/while/body/dynamic_update_slice | solution.py:111
  342.0 2.7 fusion.321
  359.1 1.5 fusion.330
  360.6 1.5 convolution_add_fusion.11
  362.0 2.5 add_multiply_fusion.3
  370.0 1.5 fusion.336
  371.5 1.5 fusion.334
  373.0 1.5 broadcast_multiply_fusion.41
  374.5 1.5 fusion.337
  379.9 6.7 %dynamic_update_slice.10 = f32[2,512,1280]{2,1,0:T(8,128)} dynamic-update-slice(f32[2,512,1280]{2,1,0:T(8,128)} %get-tuple-element.599, f32[2,256,256]{2,1,0:T(8,128)S(1)} %copy.35, s32[]{:T(128)} %constant.243.clone.1..sunk, s32[]{:T(128)S(6)} %select_n.157, s32[]{:T(128)S(6)} %select_n.158) | dynamic-update-slice | bytes 1048580 | tf_op jit(solution)/shard_map/while/body/dynamic_update_slice | solution.py:111
  391.1 4.7 slice.622
  396.5 2.0 add_dynamic-update-slice_fusion
  398.5 2.5 collective-permute-done.3
  400.9 2.0 fusion.229
  402.9 77.1 %reduce-scatter.2.cloned.1.call-done = f32[2,32,1024]{2,1,0:T(8,128)} async-done(((f32[2,512,1024]{2,1,0:T(8,128)}), f32[2,32,1024]{2,1,0:T(8,128)}) %reduce-scatter.2.cloned.1.call-update) | async-done | bytes 262160 | tf_op jit(solution)/shard_map/reduce_scatter | solution.py:119
  (294 shorter events, 158.5 us)
Async XLA Ops:
  6.5 72.4 %copy-start.1 = (s32[1,1,6]{2,1,0:T(1,128)S(1)}, s32[1,1,6]{2,1,0:T(1,128)}, u32[]{:S(2)}) copy-start(s32[1,1,6]{2,1,0:T(1,128)} %param.15) | copy-start | bytes 76
  6.5 72.4 %copy-start = (s32[1,2,96]{2,1,0:T(2,128)S(1)}, s32[1,2,96]{2,1,0:T(2,128)}, u32[]{:S(2)}) copy-start(s32[1,2,96]{2,1,0:T(2,128)} %param.14) | copy-start | bytes 2308
  6.5 69.7 %all-gather.2.cloned.1.call-start = ((), (), s32[]{:S(2)}) async-start(), calls=%async_computation.1 | async-start | bytes 5570560 | tf_op jit(solution)/shard_map/all_gather | solution.py:94
  7.3 6.4 %collective-permute-start = (f32[2,32,128]{2,1,0:T(8,128)S(1)}, f32[2,32,128]{2,1,0:T(8,128)S(1)}, u32[]{:S(2)}, u32[]{:S(2)}) collective-permute-start(f32[2,32,128]{2,1,0:T(8,128)S(1)} %get-tuple-element.418), channel_id=1, source_target_pairs={{0,1},{2,3},{4,5},{6,7},{8,9},{10,11},{12,13},{14,15},{16,17},{18,... | collective-permute-start | bytes 98312 | tf_op jit(solution)/shard_map/ppermute | solution.py:19
  12.2 5.8 %collective-permute-start.1 = (f32[2,32,128]{2,1,0:T(8,128)S(1)}, f32[2,32,128]{2,1,0:T(8,128)S(1)}, u32[]{:S(2)}, u32[]{:S(2)}) collective-permute-start(f32[2,32,128]{2,1,0:T(8,128)S(1)} %get-tuple-element.419), channel_id=1, source_target_pairs={{1,0},{3,2},{5,4},{7,6},{9,8},{11,10},{13,12},{15,14},{17,16},{19,... | collective-permute-start | bytes 98312 | tf_op jit(solution)/shard_map/ppermute | solution.py:20
  20.0 460.0 %reduce-scatter.2.cloned.1.call-start = ((), (), s32[]{:S(2)}) async-start(), calls=%async_computation.2 | async-start | bytes 4456448 | tf_op jit(solution)/shard_map/reduce_scatter | solution.py:119
  388.5 8.0 %collective-permute-start.2 = (f32[2,512,128]{2,1,0:T(8,128)S(1)}, f32[2,512,128]{2,1,0:T(8,128)S(1)}, u32[]{:S(2)}, u32[]{:S(2)}) collective-permute-start(f32[2,512,128]{2,1,0:T(8,128)S(1)} %get-tuple-element.417), channel_id=1, source_target_pairs={{0,1},{2,3},{4,5},{6,7},{8,9},{10,11},{12,13},{14,15},{16,17},{18,... | collective-permute-start | bytes 1572872 | tf_op jit(solution)/shard_map/ppermute | solution.py:19
  389.8 11.1 %collective-permute-start.3 = (f32[2,512,128]{2,1,0:T(8,128)S(1)}, f32[2,512,128]{2,1,0:T(8,128)S(1)}, u32[]{:S(2)}, u32[]{:S(2)}) collective-permute-start(f32[2,512,128]{2,1,0:T(8,128)S(1)} %get-tuple-element.416), channel_id=1, source_target_pairs={{1,0},{3,2},{5,4},{7,6},{9,8},{11,10},{13,12},{15,14},{17,16},{19,... | collective-permute-start | bytes 1572872 | tf_op jit(solution)/shard_map/ppermute | solution.py:20
Sparse Core Ops, SparseCore 0:
  20.1 56.0 all-gather.1
  403.1 76.8 reduce-scatter.1
where the time goes:
time: 489 us; the launch traced here: 487 us
  matrix products  143 us (29%)
  waiting for transfers between devices  140 us (29%)
  local copies, waits for them, and re-layouts  98 us (20%)
  other arithmetic  47.6 us (10%)
  loops' own time  36.7 us (8%)
  between operations  13.5 us (3%)
  starting transfers between devices  8.81 us (2%)
    dot_general x96, matrix products, matmul(): jnp.dot(left_side, right_side, precision=lax.Precision.HIGHEST, preferred...  143 us
    reduce_scatter x1, waiting for transfers between devices, shards(): return lax.psum_scatter(folded, 'probe', scatter_dimension=1, tiled=True)  77.1 us
    all_gather x1, waiting for transfers between devices, shards(): whole_object = lax.all_gather(widened, 'probe', axis=1, tiled=True)  54.9 us
    dynamic_update_slice x12, local copies, waits for them, and re-layouts, visit(): lax.dynamic_update_slice(gradient, current + window_grad, (anchor, start_...  40.1 us
    another operation x1, loops' own time, shards(): lax.fori_loop(0, counts[0, 0], visit, jnp.zeros(whole_object.shape, jnp.f...  36.7 us
    mul x120, other arithmetic, propagate(): term_re, term_im = (-A_PROP / degree * lap_im, A_PROP / degree * lap_re)  29.8 us
    slice x6, local copies, waits for them, and re-layouts, exit_wave(): phases = window[slice_index]  16 us
  transfers between devices with their start and end apart: 6, of which 6 were waited for; matrix products, arithmetic and copies ran while one was open for 2% of the time, Pallas kernels for 0%

commit v1 on v0

--- a/solution.py
+++ b/solution.py
@@ -7,6 +7,17 @@
 EDGE = 128
 A_PROP = 0.1
 LOSS_SCALE = 0.03125
+
+
+def around_the_ring(x, mesh_axis, dim):
+    peers = lax.axis_size(mesh_axis)
+    right = [(i, (i + 1) % peers) for i in range(peers)]
+    terms = [x]
+    for stride in range(1, peers):
+        terms = [lax.ppermute(terms[0], mesh_axis, right), *terms]
+    out = jnp.concatenate(terms, axis=dim)
+    shift = (lax.axis_index(mesh_axis) + 1) * terms[-1].shape[dim]
+    return jnp.roll(out, shift, axis=dim)
 
 
 def extended(value, sides, width):
@@ -91,7 +102,7 @@
 def shards(potential, probe_wave, offsets, members, counts, measured):
     own_width = potential.shape[2]
     widened = extended(potential, (("strip", 2),), EDGE)
-    whole_object = lax.all_gather(widened, "probe", axis=1, tiled=True)
+    whole_object = around_the_ring(widened, "probe", 1)
     window_size = probe_wave.shape[-1]
     table_re, table_im = dft_tables(window_size)
     anchor = jnp.zeros((), jnp.int32)

time: 489 us -> 614 us (1.26)
  waiting for transfers between devices: 140 us -> 213 us
  loops' own time: 36.7 us -> 59.1 us
  other arithmetic: 47.6 us -> 65.6 us
    ppermute x0 -> x15, waiting for transfers between devices: none -> 137 us  [around_the_ring(): terms = [lax.ppermute(terms[0], mesh_axis, right), *terms]]
    all_gather x1 -> x0, waiting for transfers between devices: 54.9 us -> none  [shards(): whole_object = lax.all_gather(widened, 'probe', axis=1, tiled=True)]
    another operation x1, loops' own time: 36.7 us -> 59.1 us  [shards(): lax.fori_loop(0, counts[0, 0], visit, jnp.zeros(whole_object.shape, jnp.f...]
    unnamed x5 -> x62, local copies, waits for them, and re-layouts: 1.25 us -> 13.7 us
    add x12, other arithmetic: 3.49 us -> 13 us  [exit_wave(): real_part * sine_part + imag_part * cosine]
    mul x120, other arithmetic: 29.8 us -> 38.5 us  [propagate(): term_re, term_im = (-A_PROP / degree * lap_im, A_PROP / degree * lap_re)]
    reduce_scatter x1, waiting for transfers between devices: 77.1 us -> 68.8 us  [shards(): return lax.psum_scatter(folded, 'probe', scatter_dimension=1, tiled=True)]
    slice x6, local copies, waits for them, and re-layouts: 16 us -> 8.05 us  [exit_wave(): phases = window[slice_index]]
  transfers between devices with their start and end apart: 6 -> 20, of which waited for: 6 -> 20; matrix products, arithmetic and copies ran while one was open for 2% -> 1% of each run, Pallas kernels for 0% -> 0%
where the time goes in v1:
time: 614 us; the launch traced here: 608 us
  waiting for transfers between devices  213 us (35%)
  matrix products  143 us (23%)
  local copies, waits for them, and re-layouts  104 us (17%)
  other arithmetic  65.6 us (11%)
  loops' own time  59.1 us (10%)
  between operations  14.2 us (2%)
  starting transfers between devices  8.86 us (1%)
    dot_general x96, matrix products, matmul(): jnp.dot(left_side, right_side, precision=lax.Precision.HIGHEST, preferred...  143 us
    ppermute x15, waiting for transfers between devices, around_the_ring(): terms = [lax.ppermute(terms[0], mesh_axis, right), *terms]  137 us
    reduce_scatter x1, waiting for transfers between devices, shards(): return lax.psum_scatter(folded, 'probe', scatter_dimension=1, tiled=True)  68.8 us
    another operation x1, loops' own time, shards(): lax.fori_loop(0, counts[0, 0], visit, jnp.zeros(whole_object.shape, jnp.f...  59.1 us
    dynamic_update_slice x12, local copies, waits for them, and re-layouts, visit(): lax.dynamic_update_slice(gradient, current + window_grad, (anchor, start_...  40.1 us
    mul x120, other arithmetic, propagate(): term_re, term_im = (-A_PROP / degree * lap_im, A_PROP / degree * lap_re)  38.5 us
    unnamed x62, local copies, waits for them, and re-layouts  13.7 us
    add x12, other arithmetic, exit_wave(): real_part * sine_part + imag_part * cosine  13 us
  transfers between devices with their start and end apart: 20, of which 20 were waited for; matrix products, arithmetic and copies ran while one was open for 1% of the time, Pallas kernels for 0%

profile of v1, /device:TPU:0, one launch (start us, length us, event | category | flops | bytes accessed | tf_op | source)
XLA Modules:
  0.0 607.5 jit_solution(5170646944884146478)
XLA Ops:
  7.4 4.9 collective-permute-start
  13.8 4.2 collective-permute-done.1
  19.1 9.2 %collective-permute-done.2 = f32[2,32,1280]{2,1,0:T(8,128)S(1)} collective-permute-done((f32[2,32,1280]{2,1,0:T(8,128)S(1)}, f32[2,32,1280]{2,1,0:T(8,128)S(1)}, u32[]{:S(2)}, u32[]{:S(2)}) %collective-permute-start.2) | collective-permute-done | bytes 327712 | tf_op jit(solution)/shard_map/ppermute | solution.py:17
  28.3 9.2 %collective-permute-done.3 = f32[2,32,1280]{2,1,0:T(8,128)S(1)} collective-permute-done((f32[2,32,1280]{2,1,0:T(8,128)S(1)}, f32[2,32,1280]{2,1,0:T(8,128)S(1)}, u32[]{:S(2)}, u32[]{:S(2)}) %collective-permute-start.3) | collective-permute-done | bytes 327712 | tf_op jit(solution)/shard_map/ppermute | solution.py:17
  37.5 9.2 %collective-permute-done.4 = f32[2,32,1280]{2,1,0:T(8,128)S(1)} collective-permute-done((f32[2,32,1280]{2,1,0:T(8,128)S(1)}, f32[2,32,1280]{2,1,0:T(8,128)S(1)}, u32[]{:S(2)}, u32[]{:S(2)}) %collective-permute-start.4) | collective-permute-done | bytes 327712 | tf_op jit(solution)/shard_map/ppermute | solution.py:17
  46.7 9.2 %collective-permute-done.5 = f32[2,32,1280]{2,1,0:T(8,128)S(1)} collective-permute-done((f32[2,32,1280]{2,1,0:T(8,128)S(1)}, f32[2,32,1280]{2,1,0:T(8,128)S(1)}, u32[]{:S(2)}, u32[]{:S(2)}) %collective-permute-start.5) | collective-permute-done | bytes 327712 | tf_op jit(solution)/shard_map/ppermute | solution.py:17
  55.9 9.2 %collective-permute-done.6 = f32[2,32,1280]{2,1,0:T(8,128)S(1)} collective-permute-done((f32[2,32,1280]{2,1,0:T(8,128)S(1)}, f32[2,32,1280]{2,1,0:T(8,128)S(1)}, u32[]{:S(2)}, u32[]{:S(2)}) %collective-permute-start.6) | collective-permute-done | bytes 327712 | tf_op jit(solution)/shard_map/ppermute | solution.py:17
  65.1 9.2 %collective-permute-done.7 = f32[2,32,1280]{2,1,0:T(8,128)S(1)} collective-permute-done((f32[2,32,1280]{2,1,0:T(8,128)S(1)}, f32[2,32,1280]{2,1,0:T(8,128)S(1)}, u32[]{:S(2)}, u32[]{:S(2)}) %collective-permute-start.7) | collective-permute-done | bytes 327712 | tf_op jit(solution)/shard_map/ppermute | solution.py:17
  74.3 9.2 %collective-permute-done.8 = f32[2,32,1280]{2,1,0:T(8,128)S(1)} collective-permute-done((f32[2,32,1280]{2,1,0:T(8,128)S(1)}, f32[2,32,1280]{2,1,0:T(8,128)S(1)}, u32[]{:S(2)}, u32[]{:S(2)}) %collective-permute-start.8) | collective-permute-done | bytes 327712 | tf_op jit(solution)/shard_map/ppermute | solution.py:17
  83.5 9.2 %collective-permute-done.9 = f32[2,32,1280]{2,1,0:T(8,128)S(1)} collective-permute-done((f32[2,32,1280]{2,1,0:T(8,128)S(1)}, f32[2,32,1280]{2,1,0:T(8,128)S(1)}, u32[]{:S(2)}, u32[]{:S(2)}) %collective-permute-start.9) | collective-permute-done | bytes 327712 | tf_op jit(solution)/shard_map/ppermute | solution.py:17
  92.7 9.2 %collective-permute-done.10 = f32[2,32,1280]{2,1,0:T(8,128)S(1)} collective-permute-done((f32[2,32,1280]{2,1,0:T(8,128)S(1)}, f32[2,32,1280]{2,1,0:T(8,128)S(1)}, u32[]{:S(2)}, u32[]{:S(2)}) %collective-permute-start.10) | collective-permute-done | bytes 327712 | tf_op jit(solution)/shard_map/ppermute | solution.py:17
  101.9 9.2 %collective-permute-done.11 = f32[2,32,1280]{2,1,0:T(8,128)S(1)} collective-permute-done((f32[2,32,1280]{2,1,0:T(8,128)S(1)}, f32[2,32,1280]{2,1,0:T(8,128)S(1)}, u32[]{:S(2)}, u32[]{:S(2)}) %collective-permute-start.11) | collective-permute-done | bytes 327712 | tf_op jit(solution)/shard_map/ppermute | solution.py:17
  111.8 9.2 %collective-permute-done.12 = f32[2,32,1280]{2,1,0:T(8,128)S(1)} collective-permute-done((f32[2,32,1280]{2,1,0:T(8,128)S(1)}, f32[2,32,1280]{2,1,0:T(8,128)S(1)}, u32[]{:S(2)}, u32[]{:S(2)}) %collective-permute-start.12) | collective-permute-done | bytes 327712 | tf_op jit(solution)/shard_map/ppermute | solution.py:17
  121.7 9.2 %collective-permute-done.13 = f32[2,32,1280]{2,1,0:T(8,128)S(1)} collective-permute-done((f32[2,32,1280]{2,1,0:T(8,128)S(1)}, f32[2,32,1280]{2,1,0:T(8,128)S(1)}, u32[]{:S(2)}, u32[]{:S(2)}) %collective-permute-start.13) | collective-permute-done | bytes 327712 | tf_op jit(solution)/shard_map/ppermute | solution.py:17
  131.6 9.2 %collective-permute-done.14 = f32[2,32,1280]{2,1,0:T(8,128)S(1)} collective-permute-done((f32[2,32,1280]{2,1,0:T(8,128)S(1)}, f32[2,32,1280]{2,1,0:T(8,128)S(1)}, u32[]{:S(2)}, u32[]{:S(2)}) %collective-permute-start.14) | collective-permute-done | bytes 327712 | tf_op jit(solution)/shard_map/ppermute | solution.py:17
  141.6 9.3 %collective-permute-done.15 = f32[2,32,1280]{2,1,0:T(8,128)} collective-permute-done((f32[2,32,1280]{2,1,0:T(8,128)S(1)}, f32[2,32,1280]{2,1,0:T(8,128)}, u32[]{:S(2)}, u32[]{:S(2)}) %collective-permute-start.15) | collective-permute-done | bytes 327712 | tf_op jit(solution)/shard_map/ppermute | solution.py:17
  152.2 8.2 %collective-permute-done.16 = f32[2,32,1280]{2,1,0:T(8,128)} collective-permute-done((f32[2,32,1280]{2,1,0:T(8,128)}, f32[2,32,1280]{2,1,0:T(8,128)}, u32[]{:S(2)}, u32[]{:S(2)}) %collective-permute-start.16) | collective-permute-done | bytes 327712 | tf_op jit(solution)/shard_map/ppermute | solution.py:17
  170.3 2.7 constant_dynamic-slice_fusion.5
  172.9 2.7 broadcast_in_dim.28.clone
  175.7 340.2 %while.17 = (s32[]{:T(128)}, f32[2,512,1280]{2,1,0:T(8,128)}, s32[]{:T(128)}, s32[1,1,6]{2,1,0:T(1,128)S(1)}, s32[1,2,96]{2,1,0:T(2,128)S(1)}, /*index=5*/f32[2,...) while((s32[]{:T(128)}, f32[2,512,1280]{2,1,0:T(8,128)}, ...), condition=%wide.region_1.2_spmd.clone.clone, body=%wide.region_0.1_spmd.clone.clone.sunk | while | flops 3259498496 | bytes 60293488 | solution.py:126
  210.5 2.1 fusion.325
  224.3 2.5 add_multiply_fusion.3
  233.8 1.5 broadcast_multiply_fusion.41
  235.3 1.5 fusion.336
  236.8 1.5 fusion.337
  243.7 6.6 %dynamic_update_slice.10 = f32[2,512,1280]{2,1,0:T(8,128)} dynamic-update-slice(f32[2,512,1280]{2,1,0:T(8,128)} %get-tuple-element.599, f32[2,256,256]{2,1,0:T(8,128)S(1)} %copy.34, s32[]{:T(128)} %constant.267.clone.1..sunk, s32[]{:T(128)S(6)} %select_n.171, s32[]{:T(128)S(6)} %select_n.172) | dynamic-update-slice | bytes 1048580 | tf_op jit(solution)/shard_map/while/body/dynamic_update_slice | solution.py:122
  263.6 2.1 fusion.325
  274.4 1.5 convolution_add_fusion.11
  277.4 2.5 add_multiply_fusion.3
  286.8 1.5 broadcast_multiply_fusion.41
  288.3 1.5 fusion.336
  289.8 1.5 fusion.337
  296.7 6.4 %dynamic_update_slice.10 = f32[2,512,1280]{2,1,0:T(8,128)} dynamic-update-slice(f32[2,512,1280]{2,1,0:T(8,128)} %get-tuple-element.599, f32[2,256,256]{2,1,0:T(8,128)S(1)} %copy.34, s32[]{:T(128)} %constant.267.clone.1..sunk, s32[]{:T(128)S(6)} %select_n.171, s32[]{:T(128)S(6)} %select_n.172) | dynamic-update-slice | bytes 1048580 | tf_op jit(solution)/shard_map/while/body/dynamic_update_slice | solution.py:122
  316.4 2.1 fusion.325
  327.3 1.5 convolution_add_fusion.11
  330.2 2.5 add_multiply_fusion.3
  339.7 1.5 broadcast_multiply_fusion.41
  341.2 1.5 fusion.336
  342.7 1.5 fusion.337
  349.6 6.1 %dynamic_update_slice.10 = f32[2,512,1280]{2,1,0:T(8,128)} dynamic-update-slice(f32[2,512,1280]{2,1,0:T(8,128)} %get-tuple-element.599, f32[2,256,256]{2,1,0:T(8,128)S(1)} %copy.34, s32[]{:T(128)} %constant.267.clone.1..sunk, s32[]{:T(128)S(6)} %select_n.171, s32[]{:T(128)S(6)} %select_n.172) | dynamic-update-slice | bytes 1048580 | tf_op jit(solution)/shard_map/while/body/dynamic_update_slice | solution.py:122
  369.0 2.1 fusion.325
  382.8 2.5 add_multiply_fusion.3
  392.3 1.5 broadcast_multiply_fusion.41
  393.7 1.5 fusion.336
  395.2 1.5 fusion.337
  402.2 6.7 %dynamic_update_slice.10 = f32[2,512,1280]{2,1,0:T(8,128)} dynamic-update-slice(f32[2,512,1280]{2,1,0:T(8,128)} %get-tuple-element.599, f32[2,256,256]{2,1,0:T(8,128)S(1)} %copy.34, s32[]{:T(128)} %constant.267.clone.1..sunk, s32[]{:T(128)S(6)} %select_n.171, s32[]{:T(128)S(6)} %select_n.172) | dynamic-update-slice | bytes 1048580 | tf_op jit(solution)/shard_map/while/body/dynamic_update_slice | solution.py:122
  422.2 2.1 fusion.325
  433.0 1.5 convolution_add_fusion.11
  436.0 2.5 add_multiply_fusion.3
  445.4 1.5 broadcast_multiply_fusion.41
  446.9 1.5 fusion.336
  448.4 1.5 fusion.337
  455.4 6.5 %dynamic_update_slice.10 = f32[2,512,1280]{2,1,0:T(8,128)} dynamic-update-slice(f32[2,512,1280]{2,1,0:T(8,128)} %get-tuple-element.599, f32[2,256,256]{2,1,0:T(8,128)S(1)} %copy.34, s32[]{:T(128)} %constant.267.clone.1..sunk, s32[]{:T(128)S(6)} %select_n.171, s32[]{:T(128)S(6)} %select_n.172) | dynamic-update-slice | bytes 1048580 | tf_op jit(solution)/shard_map/while/body/dynamic_update_slice | solution.py:122
  475.1 2.1 fusion.325
  488.9 2.5 add_multiply_fusion.3
  498.4 1.5 broadcast_multiply_fusion.41
  499.9 1.5 fusion.336
  501.4 1.5 fusion.337
  508.3 6.7 %dynamic_update_slice.10 = f32[2,512,1280]{2,1,0:T(8,128)} dynamic-update-slice(f32[2,512,1280]{2,1,0:T(8,128)} %get-tuple-element.599, f32[2,256,256]{2,1,0:T(8,128)S(1)} %copy.34, s32[]{:T(128)} %constant.267.clone.1..sunk, s32[]{:T(128)S(6)} %select_n.171, s32[]{:T(128)S(6)} %select_n.172) | dynamic-update-slice | bytes 1048580 | tf_op jit(solution)/shard_map/while/body/dynamic_update_slice | solution.py:122
  519.8 4.8 slice.622
  525.2 1.9 add_dynamic-update-slice_fusion
  527.1 2.5 collective-permute-done.18
  529.6 1.9 fusion.229
  531.5 68.8 %reduce-scatter.2.cloned.1.call-done = f32[2,32,1024]{2,1,0:T(8,128)} async-done(((f32[2,512,1024]{2,1,0:T(8,128)}), f32[2,32,1024]{2,1,0:T(8,128)}) %reduce-scatter.2.cloned.1.call-update) | async-done | bytes 262160 | tf_op jit(solution)/shard_map/reduce_scatter | solution.py:130
  (379 shorter events, 205.2 us)
Async XLA Ops:
  6.5 161.1 %copy-start = (f32[2,32,1024]{2,1,0:T(8,128)S(1)}, f32[2,32,1024]{2,1,0:T(8,128)}, u32[]{:S(2)}) copy-start(f32[2,32,1024]{2,1,0:T(8,128)} %param.12) | copy-start | bytes 786436
  6.5 593.8 %reduce-scatter.2.cloned.1.call-start = ((), (), s32[]{:S(2)}) async-start(), calls=%async_computation.1 | async-start | bytes 4456448 | tf_op jit(solution)/shard_map/reduce_scatter | solution.py:130
  7.4 6.4 %collective-permute-start = (f32[2,32,128]{2,1,0:T(8,128)S(1)}, f32[2,32,128]{2,1,0:T(8,128)S(1)}, u32[]{:S(2)}, u32[]{:S(2)}) collective-permute-start(f32[2,32,128]{2,1,0:T(8,128)S(1)} %get-tuple-element.418), channel_id=1, source_target_pairs={{0,1},{2,3},{4,5},{6,7},{8,9},{10,11},{12,13},{14,15},{16,17},{18,... | collective-permute-start | bytes 98312 | tf_op jit(solution)/shard_map/ppermute | solution.py:30
  12.2 5.8 collective-permute-start.1
  19.0 9.2 %collective-permute-start.2 = (f32[2,32,1280]{2,1,0:T(8,128)S(1)}, f32[2,32,1280]{2,1,0:T(8,128)S(1)}, u32[]{:S(2)}, u32[]{:S(2)}) collective-permute-start(f32[2,32,1280]{2,1,0:T(8,128)S(1)} %pad_maximum_fusion), channel_id=1, source_target_pairs={{0,2},{2,4},{4,6},{6,8},{8,10},{10,12},{12,14},{14,16},{16,18},{18... | collective-permute-start | bytes 983048 | tf_op jit(solution)/shard_map/ppermute | solution.py:17
  28.3 9.2 %collective-permute-start.3 = (f32[2,32,1280]{2,1,0:T(8,128)S(1)}, f32[2,32,1280]{2,1,0:T(8,128)S(1)}, u32[]{:S(2)}, u32[]{:S(2)}) collective-permute-start(f32[2,32,1280]{2,1,0:T(8,128)S(1)} %collective-permute-done.2), channel_id=1, source_target_pairs={{0,2},{2,4},{4,6},{6,8},{8,10},{10,12},{12,14},{14,16},{16,18},{18... | collective-permute-start | bytes 983048 | tf_op jit(solution)/shard_map/ppermute | solution.py:17
  37.5 9.2 %collective-permute-start.4 = (f32[2,32,1280]{2,1,0:T(8,128)S(1)}, f32[2,32,1280]{2,1,0:T(8,128)S(1)}, u32[]{:S(2)}, u32[]{:S(2)}) collective-permute-start(f32[2,32,1280]{2,1,0:T(8,128)S(1)} %collective-permute-done.3), channel_id=1, source_target_pairs={{0,2},{2,4},{4,6},{6,8},{8,10},{10,12},{12,14},{14,16},{16,18},{18... | collective-permute-start | bytes 983048 | tf_op jit(solution)/shard_map/ppermute | solution.py:17
  46.7 9.2 %collective-permute-start.5 = (f32[2,32,1280]{2,1,0:T(8,128)S(1)}, f32[2,32,1280]{2,1,0:T(8,128)S(1)}, u32[]{:S(2)}, u32[]{:S(2)}) collective-permute-start(f32[2,32,1280]{2,1,0:T(8,128)S(1)} %collective-permute-done.4), channel_id=1, source_target_pairs={{0,2},{2,4},{4,6},{6,8},{8,10},{10,12},{12,14},{14,16},{16,18},{18... | collective-permute-start | bytes 983048 | tf_op jit(solution)/shard_map/ppermute | solution.py:17
  55.9 9.2 %collective-permute-start.6 = (f32[2,32,1280]{2,1,0:T(8,128)S(1)}, f32[2,32,1280]{2,1,0:T(8,128)S(1)}, u32[]{:S(2)}, u32[]{:S(2)}) collective-permute-start(f32[2,32,1280]{2,1,0:T(8,128)S(1)} %collective-permute-done.5), channel_id=1, source_target_pairs={{0,2},{2,4},{4,6},{6,8},{8,10},{10,12},{12,14},{14,16},{16,18},{18... | collective-permute-start | bytes 983048 | tf_op jit(solution)/shard_map/ppermute | solution.py:17
  65.1 9.2 %collective-permute-start.7 = (f32[2,32,1280]{2,1,0:T(8,128)S(1)}, f32[2,32,1280]{2,1,0:T(8,128)S(1)}, u32[]{:S(2)}, u32[]{:S(2)}) collective-permute-start(f32[2,32,1280]{2,1,0:T(8,128)S(1)} %collective-permute-done.6), channel_id=1, source_target_pairs={{0,2},{2,4},{4,6},{6,8},{8,10},{10,12},{12,14},{14,16},{16,18},{18... | collective-permute-start | bytes 983048 | tf_op jit(solution)/shard_map/ppermute | solution.py:17
  74.3 9.2 %collective-permute-start.8 = (f32[2,32,1280]{2,1,0:T(8,128)S(1)}, f32[2,32,1280]{2,1,0:T(8,128)S(1)}, u32[]{:S(2)}, u32[]{:S(2)}) collective-permute-start(f32[2,32,1280]{2,1,0:T(8,128)S(1)} %collective-permute-done.7), channel_id=1, source_target_pairs={{0,2},{2,4},{4,6},{6,8},{8,10},{10,12},{12,14},{14,16},{16,18},{18... | collective-permute-start | bytes 983048 | tf_op jit(solution)/shard_map/ppermute | solution.py:17
  83.5 9.2 %collective-permute-start.9 = (f32[2,32,1280]{2,1,0:T(8,128)S(1)}, f32[2,32,1280]{2,1,0:T(8,128)S(1)}, u32[]{:S(2)}, u32[]{:S(2)}) collective-permute-start(f32[2,32,1280]{2,1,0:T(8,128)S(1)} %collective-permute-done.8), channel_id=1, source_target_pairs={{0,2},{2,4},{4,6},{6,8},{8,10},{10,12},{12,14},{14,16},{16,18},{18... | collective-permute-start | bytes 983048 | tf_op jit(solution)/shard_map/ppermute | solution.py:17
  92.7 9.2 %collective-permute-start.10 = (f32[2,32,1280]{2,1,0:T(8,128)S(1)}, f32[2,32,1280]{2,1,0:T(8,128)S(1)}, u32[]{:S(2)}, u32[]{:S(2)}) collective-permute-start(f32[2,32,1280]{2,1,0:T(8,128)S(1)} %collective-permute-done.9), channel_id=1, source_target_pairs={{0,2},{2,4},{4,6},{6,8},{8,10},{10,12},{12,14},{14,16},{16,18},{18... | collective-permute-start | bytes 983048 | tf_op jit(solution)/shard_map/ppermute | solution.py:17
  101.9 49.0 %copy-start.1 = (f32[2,32,1280]{2,1,0:T(8,128)}, f32[2,32,1280]{2,1,0:T(8,128)S(1)}, u32[]{:S(2)}) copy-start(f32[2,32,1280]{2,1,0:T(8,128)S(1)} %collective-permute-done.10) | copy-start | bytes 983044
  101.9 9.2 %collective-permute-start.11 = (f32[2,32,1280]{2,1,0:T(8,128)S(1)}, f32[2,32,1280]{2,1,0:T(8,128)S(1)}, u32[]{:S(2)}, u32[]{:S(2)}) collective-permute-start(f32[2,32,1280]{2,1,0:T(8,128)S(1)} %collective-permute-done.10), channel_id=1, source_target_pairs={{0,2},{2,4},{4,6},{6,8},{8,10},{10,12},{12,14},{14,16},{16,18},{18... | collective-permute-start | bytes 983048 | tf_op jit(solution)/shard_map/ppermute | solution.py:17
  111.1 0.7 copy-start.3
  111.8 9.2 %collective-permute-start.12 = (f32[2,32,1280]{2,1,0:T(8,128)S(1)}, f32[2,32,1280]{2,1,0:T(8,128)S(1)}, u32[]{:S(2)}, u32[]{:S(2)}) collective-permute-start(f32[2,32,1280]{2,1,0:T(8,128)S(1)} %collective-permute-done.11), channel_id=1, source_target_pairs={{0,2},{2,4},{4,6},{6,8},{8,10},{10,12},{12,14},{14,16},{16,18},{18... | collective-permute-start | bytes 983048 | tf_op jit(solution)/shard_map/ppermute | solution.py:17
  121.0 0.7 copy-start.5
  121.7 9.2 %collective-permute-start.13 = (f32[2,32,1280]{2,1,0:T(8,128)S(1)}, f32[2,32,1280]{2,1,0:T(8,128)S(1)}, u32[]{:S(2)}, u32[]{:S(2)}) collective-permute-start(f32[2,32,1280]{2,1,0:T(8,128)S(1)} %collective-permute-done.12), channel_id=1, source_target_pairs={{0,2},{2,4},{4,6},{6,8},{8,10},{10,12},{12,14},{14,16},{16,18},{18... | collective-permute-start | bytes 983048 | tf_op jit(solution)/shard_map/ppermute | solution.py:17
  130.9 0.7 copy-start.7
  131.6 9.2 %collective-permute-start.14 = (f32[2,32,1280]{2,1,0:T(8,128)S(1)}, f32[2,32,1280]{2,1,0:T(8,128)S(1)}, u32[]{:S(2)}, u32[]{:S(2)}) collective-permute-start(f32[2,32,1280]{2,1,0:T(8,128)S(1)} %collective-permute-done.13), channel_id=1, source_target_pairs={{0,2},{2,4},{4,6},{6,8},{8,10},{10,12},{12,14},{14,16},{16,18},{18... | collective-permute-start | bytes 983048 | tf_op jit(solution)/shard_map/ppermute | solution.py:17
  140.8 0.7 copy-start.9
  141.6 9.3 %collective-permute-start.15 = (f32[2,32,1280]{2,1,0:T(8,128)S(1)}, f32[2,32,1280]{2,1,0:T(8,128)}, u32[]{:S(2)}, u32[]{:S(2)}) collective-permute-start(f32[2,32,1280]{2,1,0:T(8,128)S(1)} %collective-permute-done.14), channel_id=1, source_target_pairs={{0,2},{2,4},{4,6},{6,8},{8,10},{10,12},{12,14},{14,16},{16,18},{18... | collective-permute-start | bytes 983048 | tf_op jit(solution)/shard_map/ppermute | solution.py:17
  150.9 9.5 %collective-permute-start.16 = (f32[2,32,1280]{2,1,0:T(8,128)}, f32[2,32,1280]{2,1,0:T(8,128)}, u32[]{:S(2)}, u32[]{:S(2)}) collective-permute-start(f32[2,32,1280]{2,1,0:T(8,128)} %collective-permute-done.15), channel_id=1, source_target_pairs={{0,2},{2,4},{4,6},{6,8},{8,10},{10,12},{12,14},{14,16},{16,18},{18... | collective-permute-start | bytes 983048 | tf_op jit(solution)/shard_map/ppermute | solution.py:17
  152.1 17.6 %copy-start.10 = (f32[2,32,1280]{2,1,0:T(8,128)S(1)}, f32[2,32,1280]{2,1,0:T(8,128)}, u32[]{:S(2)}) copy-start(f32[2,32,1280]{2,1,0:T(8,128)} %copy-done.9) | copy-start | bytes 983044
  152.1 17.6 %copy-start.8 = (f32[2,32,1280]{2,1,0:T(8,128)S(1)}, f32[2,32,1280]{2,1,0:T(8,128)}, u32[]{:S(2)}) copy-start(f32[2,32,1280]{2,1,0:T(8,128)} %copy-done.7) | copy-start | bytes 983044
  152.2 17.6 %copy-start.6 = (f32[2,32,1280]{2,1,0:T(8,128)S(1)}, f32[2,32,1280]{2,1,0:T(8,128)}, u32[]{:S(2)}) copy-start(f32[2,32,1280]{2,1,0:T(8,128)} %copy-done.5) | copy-start | bytes 983044
  152.2 17.7 %copy-start.4 = (f32[2,32,1280]{2,1,0:T(8,128)S(1)}, f32[2,32,1280]{2,1,0:T(8,128)}, u32[]{:S(2)}) copy-start(f32[2,32,1280]{2,1,0:T(8,128)} %copy-done.3) | copy-start | bytes 983044
  152.2 17.7 %copy-start.2 = (f32[2,32,1280]{2,1,0:T(8,128)S(1)}, f32[2,32,1280]{2,1,0:T(8,128)}, u32[]{:S(2)}) copy-start(f32[2,32,1280]{2,1,0:T(8,128)} %copy-done.1) | copy-start | bytes 983044
  169.9 5.7 copy-start.11
  170.0 5.7 copy-start.12
  517.2 8.0 %collective-permute-start.17 = (f32[2,512,128]{2,1,0:T(8,128)S(1)}, f32[2,512,128]{2,1,0:T(8,128)S(1)}, u32[]{:S(2)}, u32[]{:S(2)}) collective-permute-start(f32[2,512,128]{2,1,0:T(8,128)S(1)} %get-tuple-element.417), channel_id=1, source_target_pairs={{0,1},{2,3},{4,5},{6,7},{8,9},{10,11},{12,13},{14,15},{16,17},{18,... | collective-permute-start | bytes 1572872 | tf_op jit(solution)/shard_map/ppermute | solution.py:30
  518.5 11.1 %collective-permute-start.18 = (f32[2,512,128]{2,1,0:T(8,128)S(1)}, f32[2,512,128]{2,1,0:T(8,128)S(1)}, u32[]{:S(2)}, u32[]{:S(2)}) collective-permute-start(f32[2,512,128]{2,1,0:T(8,128)S(1)} %get-tuple-element.416), channel_id=1, source_target_pairs={{1,0},{3,2},{5,4},{7,6},{9,8},{11,10},{13,12},{15,14},{17,16},{19,... | collective-permute-start | bytes 1572872 | tf_op jit(solution)/shard_map/ppermute | solution.py:31
Sparse Core Ops, SparseCore 0:
  531.6 68.6 reduce-scatter.1
